TPU v7x, 768 devices: a whole 4x8x12 slice. The times are simulated.
768 devices in a mesh: tm: 32 (over x, z_hi, core), dp: 24 (over z_lo, y).
Axes of the slice: x: 4, y: 8, z: 12 (z_hi: 4, z_lo: 3; z = z_hi * 3 + z_lo), core: 2. Of those that a mesh axis runs over, the one named last changes fastest.
Arguments:
- frames_in: bfloat16 [24, 4096, 1024], P('dp', 'tm'), may hold values from -6 to 6
- valid_frames: int32 [24], P('dp'), may hold values from 2048 to 4096, as said below
- kernel: float32 [9, 1024], replicated, may hold values from -2 to 2
- w_qkv: bfloat16 [1024, 3072], replicated, may hold values from -0.1875 to 0.1875
- cotangent: bfloat16 [24, 4096, 1024], P('dp', 'tm'), may hold values from -6 to 6
Outputs:
- attended: bfloat16 [24, 4096, 1024], P('dp', 'tm')
- grad_in: bfloat16 [24, 4096, 1024], P('dp', 'tm')
- qkv_grad: float32 [24, 128, 1024], P('dp', None, 'tm')
Inputs may be any that keep to these rules, and one draw needn't show every extreme that they name: `valid_frames`: valid frames of each recording, counted from its start; some recording has all 4096 and some exactly 2048.
All inputs are finite; a program needn't handle non-finite values.
Results may differ from a plain program's by a relative error of at most 0.025.
Values may be sent and summed in bfloat16 or wider, within the bound.
A program may use at most 64 MiB of HBM per device.

v0:
```python
import functools

import jax
import jax.numpy as jnp
from jax import lax
from jax.experimental import pallas as pl
from jax.experimental.pallas import tpu as pltpu
from jax.sharding import PartitionSpec as P

HEADS = 8
HEAD = 128
KERNEL = 9
LEFT = 70
HALO = 80
FRAMES = 128
WIDTH = 1024
EXT = HALO + FRAMES + HALO
AHEAD = FRAMES + HALO
GROWS = FRAMES + 16
PAIRS = HEADS // 2
PAIR = 2 * HEAD
SECTION = 3 * PAIR

NX, NY, NZ, NZ_LO = 4, 8, 12, 3
NZ_HI = NZ // NZ_LO
MESH = pl.DeviceIdType.MESH


def dot_nn(a, b):
    return lax.dot_general(a, b, (((1,), (0,)), ((), ())), preferred_element_type=jnp.float32)


def dot_nt(a, b):
    return lax.dot_general(a, b, (((1,), (1,)), ((), ())), preferred_element_type=jnp.float32)


def dot_tn(a, b):
    return lax.dot_general(a, b, (((0,), (0,)), ((), ())), preferred_element_type=jnp.float32)


def step_kernel(
    scale, count_ref, x_hbm, c_hbm, taps_ref, w_hbm,
    att_ref, gin_ref, out_ref,
    x_own, c_own, xp, xn, cn, ext, hid, slope, cot, mask_own, mask_next, wbuf, qkv, near, gq, gh, gc,
    ht_own, ht_prev, hr_own, hr_prev, g_own, g_prev, gr_own, gr_prev,
    wa, wb, r_ax, r_by, r_ay, r_bx, r_az, r_bz, local, send, recv,
):
    tm, dp = lax.axis_index("tm"), lax.axis_index("dp")
    steps = lax.axis_size("tm")
    core = lax.rem(tm, 2)
    zh = lax.rem(tm // 2, NZ_HI)
    x = tm // (2 * NZ_HI)
    y = lax.rem(dp, NY)
    zl = dp // NY
    z = zh * NZ_LO + zl
    begin = tm * FRAMES
    count = count_ref[0]
    factor = HEAD ** (-0.5)

    def device(x, y, z, core):
        return {"tm": (x * NZ_HI + z // NZ_LO) * 2 + core, "dp": lax.rem(z, NZ_LO) * NY + y}

    after, before = {"tm": lax.rem(tm + 1, steps)}, {"tm": lax.rem(tm + steps - 1, steps)}
    partner = device(x, y, z, 1 - core)
    near_by = {
        ("x", 1): device(lax.rem(x + 1, NX), y, z, core),
        ("x", -1): device(lax.rem(x + NX - 1, NX), y, z, core),
        ("y", 1): device(x, lax.rem(y + 1, NY), z, core),
        ("y", -1): device(x, lax.rem(y + NY - 1, NY), z, core),
    }
    column = [device(x, y, lax.rem(z + k, NZ), core) for k in range(1, NZ)]

    barrier = pltpu.get_barrier_semaphore()
    peers = [after, before, *near_by.values(), *column]
    for other in peers:
        pl.semaphore_signal(barrier, inc=1, device_id=other, device_id_type=MESH)

    order = [lax.rem(y // 2 + turn, PAIRS) for turn in (2, 1, 3, 0)]

    def weight(pair, section):
        return pltpu.make_async_copy(
            w_hbm.at[:, pl.ds(section * WIDTH + pair * PAIR, PAIR)],
            wbuf.at[pair, :, pl.ds(section * PAIR, PAIR)],
            local.at[2 + pair * 3 + section],
        )

    own = [
        pltpu.make_async_copy(x_hbm.at[0], x_own, local.at[0]),
        pltpu.make_async_copy(c_hbm.at[0], c_own, local.at[1]),
    ]
    for one in own:
        one.start()
    for pair in order:
        for section in range(3):
            weight(pair, section).start()

    pl.semaphore_wait(barrier, len(peers))

    slots = iter(range(SLOTS))
    sent = []

    def start(source, target, other):
        slot = next(slots)
        one = pltpu.make_async_remote_copy(
            src_ref=source,
            dst_ref=target,
            send_sem=send.at[slot],
            recv_sem=recv.at[slot],
            device_id=other,
            device_id_type=MESH,
        )
        one.start()
        sent.append(one)
        return one

    got_xp = start(x_hbm.at[0, pl.ds(FRAMES - HALO, HALO)], xp, after)
    got_xn = start(x_hbm.at[0, pl.ds(0, HALO)], xn, before)
    got_cn = start(c_hbm.at[0, pl.ds(0, HALO)], cn, before)

    def live_rows(first, rows):
        at = first + lax.broadcasted_iota(jnp.int32, (rows, 1), 0)
        return (at >= 0) & (at < count)

    def masked(first, value):
        return jnp.where(live_rows(first, value.shape[0]), value.astype(jnp.float32), 0.0)

    def band(rows, columns, first_query, first_key):
        query = first_query + lax.broadcasted_iota(jnp.int32, (rows, columns), 0)
        key = first_key + lax.broadcasted_iota(jnp.int32, (rows, columns), 1)
        offset = query - key
        allowed = (offset >= 0) & (offset <= LEFT) & (key >= 0) & (key < count) & (query < count)
        return jnp.where(allowed, 1.0, 0.0)

    def conv_rows(step, _):
        row = pl.multiple_of(step * 16, 16)
        window = ext[pl.ds(row, 24), :]
        total = jnp.zeros((16, WIDTH), jnp.float32)
        for tap in range(KERNEL):
            total = total + taps_ref[tap : tap + 1, :] * window[tap : tap + 16]
        logistic = 1.0 / (1.0 + jnp.exp(-total))
        hid[pl.ds(row, 16), :] = (window[8:24] + total * logistic).astype(jnp.bfloat16)
        slope[pl.ds(row, 16), :] = logistic * (1.0 + total * (1.0 - logistic))
        return 0

    def turn(first, take, target):
        for block in range(WIDTH // 128):
            tile = hid[first : first + FRAMES, block * 128 : (block + 1) * 128]
            turned = tile.astype(jnp.float32).T.astype(jnp.bfloat16)
            for piece in range(8):
                group = block * 2 + piece // 4
                rows = piece % 2 * (WIDTH // 4) + group * 16
                target[(piece // 2) % 2, rows : rows + 16, :] = turned[piece * 16 : (piece + 1) * 16, 0:take]

    inner = HALO + 16
    ext[0:8, :] = jnp.zeros((8, WIDTH), jnp.float32)
    mask_own[...] = band(FRAMES, AHEAD, begin, begin - HALO)
    mask_next[...] = band(HALO, 2 * HALO, begin + FRAMES, begin + FRAMES - HALO)
    own[0].wait()
    ext[8 + HALO : 8 + AHEAD, :] = masked(begin, x_own[...])
    lax.fori_loop(inner // 16, AHEAD // 16, conv_rows, 0)
    own[1].wait()
    cot[0:FRAMES, :] = masked(begin, c_own[...]).astype(jnp.bfloat16)
    for pair in order:
        for section in range(3):
            weight(pair, section).wait()
        qkv[pair, inner:AHEAD, :] = dot_nn(hid[inner:AHEAD, :], wbuf[pair]).astype(jnp.bfloat16)

    got_xp.wait_recv()
    ext[8 : 8 + HALO, :] = masked(begin - HALO, xp[...])
    lax.fori_loop(0, inner // 16, conv_rows, 0)
    turn(HALO, FRAMES, ht_own)
    turn(0, HALO, ht_prev)
    got_h = [start(ht_own.at[1 - core], hr_own, partner), start(ht_prev.at[1 - core], hr_prev, partner)]

    def attend(q, g, k, v, mask, first):
        raised = jnp.where(mask > 0.5, jnp.exp(dot_nt(q, k) * factor), 0.0)
        at = first + lax.broadcasted_iota(jnp.int32, (q.shape[0], 1), 0)
        missing = jnp.where(at < count, 0.0, 1.0)
        prob = raised * (1.0 / (jnp.sum(raised, axis=1, keepdims=True) + missing))
        grad_prob = dot_nt(g, v)
        mean = jnp.sum(prob * grad_prob, axis=1, keepdims=True)
        grad_score = (prob * (grad_prob - mean) * factor).astype(jnp.bfloat16)
        return prob.astype(jnp.bfloat16), grad_score

    def section_at(section, head):
        return slice(section * PAIR + head * HEAD, section * PAIR + (head + 1) * HEAD)

    def lanes(pair, head):
        return pl.ds(pl.multiple_of(pair * PAIR + head * HEAD, HEAD), HEAD)

    def attend_own(turn_no):
        pair = order[turn_no]
        qkv[pair, 0:inner, :] = dot_nn(hid[0:inner, :], wbuf[pair]).astype(jnp.bfloat16)
        for head in range(2):
            q = qkv[pair, HALO:AHEAD, section_at(0, head)]
            k = qkv[pair, 0:AHEAD, section_at(1, head)]
            v = qkv[pair, 0:AHEAD, section_at(2, head)]
            g = cot[0:FRAMES, lanes(pair, head)]
            prob, score = attend(q, g, k, v, mask_own[...], begin)
            att_ref[0, :, lanes(pair, head)] = dot_nn(prob, v).astype(jnp.bfloat16)
            g_own[turn_no, :, section_at(0, head)] = dot_nn(score, k).astype(jnp.bfloat16)
            for section, left, right in ((1, score, q), (2, prob, g)):
                total = dot_tn(left, right)
                g_prev[turn_no, :, section_at(section - 1, head)] = total[0:HALO].astype(jnp.bfloat16)
                g_own[turn_no, :, section_at(section, head)] = total[HALO:AHEAD].astype(jnp.bfloat16)
                near[turn_no, :, section_at(section - 1, head)] = total[HALO:AHEAD]
        return [
            start(g_own.at[turn_no], gr_own.at[turn_no], partner),
            start(g_prev.at[turn_no], gr_prev.at[turn_no], partner),
        ]

    def products(turn_no, landed):
        for one in landed:
            one.wait_recv()
        pair = order[turn_no]
        for section in range(3):
            at = slice(section * PAIR, (section + 1) * PAIR)
            if section == 0:
                left = jnp.concatenate([ht_own[core], hr_own[...]], axis=1)
                right = jnp.concatenate([g_own[turn_no, :, at], gr_own[turn_no, :, at]], axis=0)
                product = dot_nn(left, right)
            else:
                low = slice((section - 1) * PAIR, section * PAIR)
                product = dot_nn(
                    jnp.concatenate([ht_own[core], ht_prev[core]], axis=1),
                    jnp.concatenate([g_own[turn_no, :, at], g_prev[turn_no, :, low]], axis=0),
                ) + dot_nn(
                    jnp.concatenate([hr_own[...], hr_prev[...]], axis=1),
                    jnp.concatenate([gr_own[turn_no, :, at], gr_prev[turn_no, :, low]], axis=0),
                )
            product = product.astype(jnp.bfloat16)
            for part in range(2):
                for row in range(NX):
                    for high in range(NZ_HI):
                        first = ((part * NX + row) * NZ_HI + high) * 16
                        for head in range(2):
                            value = product[first : first + 16, head * HEAD : (head + 1) * HEAD]
                            if part == 0:
                                wa[row, pair * 2 + head, high * NZ_LO + section] = value
                            else:
                                wb[pair * 2 + head, row, high * NZ_LO + section] = value

    def add_into(ref, landed):
        total = ref[...].astype(jnp.float32)
        for one in landed:
            total = total + one[...].astype(jnp.float32)
        ref[...] = total.astype(jnp.bfloat16)

    class Chain:
        def __init__(self, axis, size, at, way, length, block, landing):
            self.to, self.size, self.at, self.way, self.length = near_by[axis, way], size, at, way, length
            self.block, self.landing, self.done, self.pending = block, landing, 0, None

        def step(self):
            self.done += 1
            place = lax.rem(self.at + self.size + self.way * (self.length - self.done + 1), self.size)
            ref = self.block(place)
            if self.pending is not None:
                self.pending.wait_recv()
                add_into(ref, [self.landing(self.done - 2)])
            self.pending = start(ref, self.landing(self.done - 1), self.to)

        def last(self):
            self.pending.wait_recv()
            return self.landing(self.length - 1)

    def half(ref, which, size):
        return ref.at[pl.ds(which * (size // 2), size // 2)]

    def four(axis, size, at, block, landing):
        far, less = size // 2, size // 2 - 1
        chains, slot = [], 0
        for way, which, length in ((1, 0, far), (-1, 1, far), (1, 1, less), (-1, 0, less)):
            chains.append(
                Chain(axis, size, at, way, length,
                      lambda place, which=which: block(place, which),
                      lambda step, slot=slot: landing.at[slot + step])
            )
            slot += length
        return chains

    def finish_four(chains, block, at):
        add_into(block(at, 0), [chains[0].last(), chains[3].last()])
        add_into(block(at, 1), [chains[1].last(), chains[2].last()])

    ax = []
    for turn_no in range(PAIRS):
        def head_block(place, which, turn_no=turn_no):
            return wa.at[place, order[turn_no] * 2 + which]
        ax.append((four("x", NX, x, head_block, r_ax.at[turn_no]), head_block))

    def by_block(place, which):
        return half(wb.at[place], which, NX)

    def ay_block(place, which):
        return half(wa.at[x, place], which, NZ)

    def bx_block(place, which):
        return half(wb.at[y, place], which, NZ)

    by = four("y", NY, y, by_block, r_by)
    ay = four("y", NY, y, ay_block, r_ay)
    bx = four("x", NX, x, bx_block, r_bx)

    def step_all(chains, which):
        for index in which:
            chains[index].step()

    def attend_next(turn_no):
        pair = order[turn_no]
        qkv[pair, AHEAD:EXT, :] = dot_nn(hid[AHEAD:EXT, :], wbuf[pair]).astype(jnp.bfloat16)
        gq[0:FRAMES, 0:PAIR] = g_own[turn_no, :, 0:PAIR]
        for head in range(2):
            q = qkv[pair, AHEAD:EXT, section_at(0, head)]
            k = qkv[pair, FRAMES:EXT, section_at(1, head)]
            v = qkv[pair, FRAMES:EXT, section_at(2, head)]
            g = cot[FRAMES:AHEAD, lanes(pair, head)]
            prob, score = attend(q, g, k, v, mask_next[...], begin + FRAMES)
            gq[FRAMES:GROWS, section_at(0, head)] = dot_nn(score[0:16], k).astype(jnp.bfloat16)
            split = FRAMES - HALO
            for section, left, right in ((1, score, q), (2, prob, g)):
                far = dot_tn(left, right)
                at = section_at(section, head)
                mine = near.at[turn_no, :, section_at(section - 1, head)]
                gq[0:split, at] = mine[0:split].astype(jnp.bfloat16)
                gq[split:FRAMES, at] = (mine[split:FRAMES] + far[0:HALO]).astype(jnp.bfloat16)
                gq[FRAMES:GROWS, at] = far[HALO : HALO + 16].astype(jnp.bfloat16)
        gh[...] += dot_nt(gq[...], wbuf[pair])

    def conv_next():
        got_xn.wait_recv()
        ext[8 + AHEAD : 8 + EXT, :] = masked(begin + FRAMES, xn[...])
        lax.fori_loop(AHEAD // 16, EXT // 16, conv_rows, 0)
        got_cn.wait_recv()
        cot[FRAMES:AHEAD, :] = masked(begin + FRAMES, cn[...]).astype(jnp.bfloat16)
        gh[...] = jnp.zeros_like(gh)

    def spread_rows(step, _):
        row = pl.multiple_of(step * 16, 16)
        total = gh[pl.ds(row, 16), :]
        window = gc[pl.ds(row, 24), :]
        for tap in range(KERNEL):
            total = total + taps_ref[tap : tap + 1, :] * window[8 - tap : 24 - tap]
        gin_ref[0, pl.ds(row, 16), :] = jnp.where(live_rows(begin + row, 16), total, 0.0).astype(jnp.bfloat16)
        return 0

    def spread():
        gc[...] = gh[...] * slope[HALO : HALO + GROWS, :]
        lax.fori_loop(0, FRAMES // 16, spread_rows, 0)

    def send_column(block, landing):
        return [
            start(block.at[lax.rem(z + k, NZ)], landing.at[k - 1], column[k - 1]) for k in range(1, NZ)
        ]

    def finish(part, own_block, landing, landed):
        total = own_block[z].astype(jnp.float32)
        for index, one in enumerate(landed):
            one.wait_recv()
            total = total + landing[index].astype(jnp.float32)
        out_ref[part * 16 : (part + 1) * 16, :] = total * scale

    sent_0 = attend_own(0)
    sent_1 = attend_own(1)
    for one in got_h:
        one.wait_recv()
    products(0, sent_0)
    step_all(ax[0][0], (0, 1, 2, 3))
    step_all(by, (0, 1))
    sent_2 = attend_own(2)
    products(1, sent_1)
    step_all(ax[1][0], (0, 1, 2, 3))
    step_all(by, (0, 2))
    step_all(ax[0][0], (0, 1))
    sent_3 = attend_own(3)
    products(2, sent_2)
    step_all(ax[2][0], (0, 1, 2, 3))
    step_all(by, (1, 3, 0, 2))
    step_all(ax[1][0], (0, 1))
    products(3, sent_3)
    step_all(ax[3][0], (0, 1, 2, 3))
    step_all(by, (1, 3, 0, 2))
    step_all(ax[2][0], (0, 1))
    conv_next()
    attend_next(0)
    step_all(ax[3][0], (0, 1))
    step_all(by, (1, 3))
    attend_next(1)
    attend_next(2)
    for chains, block in ax:
        finish_four(chains, block, x)
    step_all(ay, (0, 1, 2, 3))
    attend_next(3)
    finish_four(by, by_block, y)
    step_all(bx, (0, 1, 2, 3))
    step_all(ay, (0, 1, 2, 3))
    spread()
    step_all(bx, (0, 1))
    step_all(ay, (0, 1, 2, 3))
    finish_four(bx, bx_block, x)
    got_b = send_column(wb.at[y, x], r_bz)
    step_all(ay, (0, 1))
    finish_four(ay, ay_block, y)
    got_a = send_column(wa.at[x, y], r_az)
    finish(1, wb.at[y, x], r_bz, got_b)
    finish(0, wa.at[x, y], r_az, got_a)
    for one in sent:
        one.wait_send()


SLOTS = 112


def whole_step(frames_in, valid_frames, taps, w_qkv, cotangent):
    vmem, anywhere = pl.BlockSpec(memory_space=pltpu.VMEM), pl.BlockSpec(memory_space=pl.ANY)
    bf16, f32 = jnp.bfloat16, jnp.float32
    rows = jax.ShapeDtypeStruct((1, FRAMES, WIDTH), bf16)
    scale = float(lax.axis_size("dp") * lax.axis_size("tm") * FRAMES) ** (-0.5)
    scratch = [
        ((FRAMES, WIDTH), bf16), ((FRAMES, WIDTH), bf16),
        ((HALO, WIDTH), bf16), ((HALO, WIDTH), bf16), ((HALO, WIDTH), bf16),
        ((EXT + 8, WIDTH), f32), ((EXT, WIDTH), bf16), ((EXT, WIDTH), f32), ((AHEAD, WIDTH), bf16),
        ((FRAMES, AHEAD), f32), ((HALO, 2 * HALO), f32),
        ((PAIRS, WIDTH, SECTION), bf16), ((PAIRS, EXT, SECTION), bf16), ((PAIRS, FRAMES, 2 * PAIR), f32),
        ((GROWS, SECTION), bf16), ((GROWS, WIDTH), f32), ((GROWS, WIDTH), f32),
        ((2, WIDTH // 2, FRAMES), bf16), ((2, WIDTH // 2, HALO), bf16),
        ((WIDTH // 2, FRAMES), bf16), ((WIDTH // 2, HALO), bf16),
        ((PAIRS, FRAMES, SECTION), bf16), ((PAIRS, HALO, 2 * PAIR), bf16),
        ((PAIRS, FRAMES, SECTION), bf16), ((PAIRS, HALO, 2 * PAIR), bf16),
        ((NX, NY, NZ, 16, HEAD), bf16), ((NY, NX, NZ, 16, HEAD), bf16),
        ((PAIRS, 6, NZ, 16, HEAD), bf16), ((14, NX // 2, NZ, 16, HEAD), bf16),
        ((14, NZ // 2, 16, HEAD), bf16), ((6, NZ // 2, 16, HEAD), bf16),
        ((NZ - 1, 16, HEAD), bf16), ((NZ - 1, 16, HEAD), bf16),
    ]
    return pl.pallas_call(
        functools.partial(step_kernel, scale),
        out_shape=(rows, rows, jax.ShapeDtypeStruct((32, HEAD), f32)),
        in_specs=[pl.BlockSpec(memory_space=pltpu.SMEM), anywhere, anywhere, vmem, anywhere],
        out_specs=(vmem, vmem, vmem),
        scratch_shapes=[pltpu.VMEM(shape, kind) for shape, kind in scratch]
        + [pltpu.SemaphoreType.DMA((2 + 3 * PAIRS,)), pltpu.SemaphoreType.DMA((SLOTS,)), pltpu.SemaphoreType.DMA((SLOTS,))],
        compiler_params=pltpu.CompilerParams(
            collective_id=0, has_side_effects=True, vmem_limit_bytes=60 * 1024 * 1024
        ),
        name="step",
    )(valid_frames, frames_in, cotangent, taps, w_qkv)


def on_device(frames_in, valid_frames, kernel, w_qkv, cotangent):
    attended, grad_in, block = whole_step(frames_in, valid_frames, kernel, w_qkv, cotangent)
    return (attended, grad_in, block.T[None])


def solution(mesh):
    return jax.shard_map(
        on_device,
        mesh=mesh,
        in_specs=(P("dp", "tm", None), P("dp"), P(), P(), P("dp", "tm", None)),
        out_specs=(P("dp", "tm", None), P("dp", "tm", None), P("dp", None, "tm")),
        check_vma=False,
    )
```

profile of v0, /device:TPU:2, one launch (start us, length us, event | category | flops | bytes accessed | tf_op | source)
XLA Modules:
  0.0 80.9 jit_solution(17301615146053589833)
XLA Ops:
  1.3 75.0 %step.1 = (bf16[1,128,1024]{2,1,0:T(8,128)(2,1)}, bf16[1,128,1024]{2,1,0:T(8,128)(2,1)}, f32[32,128]{1,0:T(8,128)}) custom-call(s32[1]{0:T(128)S(6)} %copy.11.count_ref, bf16[1,128,1024]{2,1,0:T(8,128)(2,1)} %x_hbm.1, bf16[1,128,1024]{2,1,0:T(8,128)(2,1)} %c_hbm.1, f32[9,1024]{1,0:T(8,128)} %taps_ref.1, bf16[1024,3072]{1,0:T(8,128)(2,1)} %w_hbm.1), custom_call_target="tpu_custom_call" | custom-call | tf_op jit(solution)/shard_map/step/pallas_call | solution.py:435
  76.3 1.7 %copy.12 = bf16[1,128,1024]{2,1,0:T(8,128)(2,1)} copy(bf16[1,128,1024]{2,1,0:T(8,128)(2,1)} %get-tuple-element.12) | data formatting | bytes 524288
  77.9 1.7 %copy.13 = bf16[1,128,1024]{2,1,0:T(8,128)(2,1)} copy(bf16[1,128,1024]{2,1,0:T(8,128)(2,1)} %get-tuple-element.13) | data formatting | bytes 524288
  79.6 1.3 %copy.14 = f32[1,128,32]{1,2,0:T(8,128)} copy(f32[1,128,32]{1,2,0:T(8,128)} %bitcast.3) | data formatting | bytes 32768
where the time goes:
time: 81.2 us; the launch traced here: 80.9 us
  Pallas kernels  75 us (92%)
  local copies, waits for them, and re-layouts  4.66 us (6%)
  between operations  1.29 us (2%)
    pallas_call x1, Pallas kernels, whole_step(): pl.pallas_call(functools.partial(step_kernel, scale), out_shape=(rows, ro...  75 us
    unnamed x3, local copies, waits for them, and re-layouts  4.66 us

commit v1 on v0

--- a/solution.py
+++ b/solution.py
@@ -18,6 +18,7 @@
 AHEAD = FRAMES + HALO
 GROWS = FRAMES + 16
 PAIRS = HEADS // 2
+ROWS_A, ROWS_B = 24, 8
 PAIR = 2 * HEAD
 SECTION = 3 * PAIR
 
@@ -39,9 +40,9 @@
 
 
 def step_kernel(
-    scale, count_ref, x_hbm, c_hbm, taps_ref, w_hbm,
+    scale, count_ref, x_hbm, c_hbm, taps_hbm, w_hbm,
     att_ref, gin_ref, out_ref,
-    x_own, c_own, xp, xn, cn, ext, hid, slope, cot, mask_own, mask_next, wbuf, qkv, near, gq, gh, gc,
+    taps_ref, x_own, c_own, xp, xn, cn, ext, hid, slope, cot, mask_own, mask_next, wbuf, qkv, near, gq, gh, gc,
     ht_own, ht_prev, hr_own, hr_prev, g_own, g_prev, gr_own, gr_prev,
     wa, wb, r_ax, r_by, r_ay, r_bx, r_az, r_bz, local, send, recv,
 ):
@@ -81,12 +82,13 @@
         return pltpu.make_async_copy(
             w_hbm.at[:, pl.ds(section * WIDTH + pair * PAIR, PAIR)],
             wbuf.at[pair, :, pl.ds(section * PAIR, PAIR)],
-            local.at[2 + pair * 3 + section],
+            local.at[3 + pair * 3 + section],
         )
 
     own = [
         pltpu.make_async_copy(x_hbm.at[0], x_own, local.at[0]),
         pltpu.make_async_copy(c_hbm.at[0], c_own, local.at[1]),
+        pltpu.make_async_copy(taps_hbm, taps_ref, local.at[2]),
     ]
     for one in own:
         one.start()
@@ -145,17 +147,19 @@
     def turn(first, take, target):
         for block in range(WIDTH // 128):
             tile = hid[first : first + FRAMES, block * 128 : (block + 1) * 128]
-            turned = tile.astype(jnp.float32).T.astype(jnp.bfloat16)
-            for piece in range(8):
-                group = block * 2 + piece // 4
-                rows = piece % 2 * (WIDTH // 4) + group * 16
-                target[(piece // 2) % 2, rows : rows + 16, :] = turned[piece * 16 : (piece + 1) * 16, 0:take]
+            turned = tile.astype(jnp.float32).T[:, 0:take]
+            for group in range(4):
+                place, side, row = block * 2 + group // 2, group % 2, group * 32
+                at_a, at_b = place * ROWS_A, NX * NZ_HI * ROWS_A + place * ROWS_B
+                target[side, at_a : at_a + ROWS_A, :] = turned[row : row + ROWS_A].astype(jnp.bfloat16)
+                target[side, at_b : at_b + ROWS_B, :] = turned[row + ROWS_A : row + 32].astype(jnp.bfloat16)
 
     inner = HALO + 16
     ext[0:8, :] = jnp.zeros((8, WIDTH), jnp.float32)
     mask_own[...] = band(FRAMES, AHEAD, begin, begin - HALO)
     mask_next[...] = band(HALO, 2 * HALO, begin + FRAMES, begin + FRAMES - HALO)
     own[0].wait()
+    own[2].wait()
     ext[8 + HALO : 8 + AHEAD, :] = masked(begin, x_own[...])
     lax.fori_loop(inner // 16, AHEAD // 16, conv_rows, 0)
     own[1].wait()
@@ -228,17 +232,18 @@
                     jnp.concatenate([hr_own[...], hr_prev[...]], axis=1),
                     jnp.concatenate([gr_own[turn_no, :, at], gr_prev[turn_no, :, low]], axis=0),
                 )
-            product = product.astype(jnp.bfloat16)
-            for part in range(2):
-                for row in range(NX):
-                    for high in range(NZ_HI):
-                        first = ((part * NX + row) * NZ_HI + high) * 16
-                        for head in range(2):
-                            value = product[first : first + 16, head * HEAD : (head + 1) * HEAD]
-                            if part == 0:
-                                wa[row, pair * 2 + head, high * NZ_LO + section] = value
-                            else:
-                                wb[pair * 2 + head, row, high * NZ_LO + section] = value
+            for row in range(NX):
+                for high in range(NZ_HI):
+                    place = row * NZ_HI + high
+                    at_a, at_b = place * ROWS_A, NX * NZ_HI * ROWS_A + place * ROWS_B
+                    for head in range(2):
+                        lane = slice(head * HEAD, (head + 1) * HEAD)
+                        wa[row, pair * 2 + head, high * NZ_LO + section] = product[
+                            at_a : at_a + ROWS_A, lane
+                        ].astype(jnp.bfloat16)
+                        wb[pair * 2 + head, row, high * NZ_LO + section] = product[
+                            at_b : at_b + ROWS_B, lane
+                        ].astype(jnp.bfloat16)
 
     def add_into(ref, landed):
         total = ref[...].astype(jnp.float32)
@@ -353,12 +358,16 @@
             start(block.at[lax.rem(z + k, NZ)], landing.at[k - 1], column[k - 1]) for k in range(1, NZ)
         ]
 
-    def finish(part, own_block, landing, landed):
+    def finish(rows, own_block, landing, landed):
         total = own_block[z].astype(jnp.float32)
         for index, one in enumerate(landed):
             one.wait_recv()
             total = total + landing[index].astype(jnp.float32)
-        out_ref[part * 16 : (part + 1) * 16, :] = total * scale
+        out_ref[rows, :] = total * scale
+
+    def finish_ax(turn_no):
+        chains, block = ax[turn_no]
+        finish_four(chains, block, x)
 
     sent_0 = attend_own(0)
     sent_1 = attend_own(1)
@@ -376,34 +385,38 @@
     products(2, sent_2)
     step_all(ax[2][0], (0, 1, 2, 3))
     step_all(by, (1, 3, 0, 2))
+    products(3, sent_3)
     step_all(ax[1][0], (0, 1))
-    products(3, sent_3)
     step_all(ax[3][0], (0, 1, 2, 3))
     step_all(by, (1, 3, 0, 2))
+    conv_next()
     step_all(ax[2][0], (0, 1))
-    conv_next()
+    step_all(by, (1, 3))
     attend_next(0)
+    finish_ax(0)
+    step_all(ay, (0, 1))
     step_all(ax[3][0], (0, 1))
-    step_all(by, (1, 3))
     attend_next(1)
-    attend_next(2)
-    for chains, block in ax:
-        finish_four(chains, block, x)
-    step_all(ay, (0, 1, 2, 3))
-    attend_next(3)
     finish_four(by, by_block, y)
     step_all(bx, (0, 1, 2, 3))
+    finish_ax(1)
+    step_all(ay, (0, 2))
+    attend_next(2)
+    step_all(ay, (0, 2))
+    step_all(bx, (0, 1))
+    finish_ax(2)
+    step_all(ay, (1, 3))
+    attend_next(3)
+    step_all(ay, (1, 3))
+    finish_four(bx, bx_block, x)
+    got_b = send_column(wb.at[y, x], r_bz)
+    finish_ax(3)
     step_all(ay, (0, 1, 2, 3))
     spread()
-    step_all(bx, (0, 1))
-    step_all(ay, (0, 1, 2, 3))
-    finish_four(bx, bx_block, x)
-    got_b = send_column(wb.at[y, x], r_bz)
-    step_all(ay, (0, 1))
     finish_four(ay, ay_block, y)
     got_a = send_column(wa.at[x, y], r_az)
-    finish(1, wb.at[y, x], r_bz, got_b)
-    finish(0, wa.at[x, y], r_az, got_a)
+    finish(slice(ROWS_A, ROWS_A + ROWS_B), wb.at[y, x], r_bz, got_b)
+    finish(slice(0, ROWS_A), wa.at[x, y], r_az, got_a)
     for one in sent:
         one.wait_send()
 
@@ -417,7 +430,7 @@
     rows = jax.ShapeDtypeStruct((1, FRAMES, WIDTH), bf16)
     scale = float(lax.axis_size("dp") * lax.axis_size("tm") * FRAMES) ** (-0.5)
     scratch = [
-        ((FRAMES, WIDTH), bf16), ((FRAMES, WIDTH), bf16),
+        ((KERNEL, WIDTH), f32), ((FRAMES, WIDTH), bf16), ((FRAMES, WIDTH), bf16),
         ((HALO, WIDTH), bf16), ((HALO, WIDTH), bf16), ((HALO, WIDTH), bf16),
         ((EXT + 8, WIDTH), f32), ((EXT, WIDTH), bf16), ((EXT, WIDTH), f32), ((AHEAD, WIDTH), bf16),
         ((FRAMES, AHEAD), f32), ((HALO, 2 * HALO), f32),
@@ -427,20 +440,20 @@
         ((WIDTH // 2, FRAMES), bf16), ((WIDTH // 2, HALO), bf16),
         ((PAIRS, FRAMES, SECTION), bf16), ((PAIRS, HALO, 2 * PAIR), bf16),
         ((PAIRS, FRAMES, SECTION), bf16), ((PAIRS, HALO, 2 * PAIR), bf16),
-        ((NX, NY, NZ, 16, HEAD), bf16), ((NY, NX, NZ, 16, HEAD), bf16),
-        ((PAIRS, 6, NZ, 16, HEAD), bf16), ((14, NX // 2, NZ, 16, HEAD), bf16),
-        ((14, NZ // 2, 16, HEAD), bf16), ((6, NZ // 2, 16, HEAD), bf16),
-        ((NZ - 1, 16, HEAD), bf16), ((NZ - 1, 16, HEAD), bf16),
+        ((NX, NY, NZ, ROWS_A, HEAD), bf16), ((NY, NX, NZ, ROWS_B, HEAD), bf16),
+        ((PAIRS, 6, NZ, ROWS_A, HEAD), bf16), ((14, NX // 2, NZ, ROWS_B, HEAD), bf16),
+        ((14, NZ // 2, ROWS_A, HEAD), bf16), ((6, NZ // 2, ROWS_B, HEAD), bf16),
+        ((NZ - 1, ROWS_A, HEAD), bf16), ((NZ - 1, ROWS_B, HEAD), bf16),
     ]
     return pl.pallas_call(
         functools.partial(step_kernel, scale),
         out_shape=(rows, rows, jax.ShapeDtypeStruct((32, HEAD), f32)),
-        in_specs=[pl.BlockSpec(memory_space=pltpu.SMEM), anywhere, anywhere, vmem, anywhere],
+        in_specs=[pl.BlockSpec(memory_space=pltpu.SMEM)] + [anywhere] * 4,
         out_specs=(vmem, vmem, vmem),
         scratch_shapes=[pltpu.VMEM(shape, kind) for shape, kind in scratch]
-        + [pltpu.SemaphoreType.DMA((2 + 3 * PAIRS,)), pltpu.SemaphoreType.DMA((SLOTS,)), pltpu.SemaphoreType.DMA((SLOTS,))],
+        + [pltpu.SemaphoreType.DMA((3 + 3 * PAIRS,)), pltpu.SemaphoreType.DMA((SLOTS,)), pltpu.SemaphoreType.DMA((SLOTS,))],
         compiler_params=pltpu.CompilerParams(
-            collective_id=0, has_side_effects=True, vmem_limit_bytes=60 * 1024 * 1024
+            collective_id=0, has_side_effects=True, vmem_limit_bytes=54500 * 1024
         ),
         name="step",
     )(valid_frames, frames_in, cotangent, taps, w_qkv)

time: 81.2 us -> 77.9 us (0.959)
  the two profiles are of different devices: /device:TPU:2 before, /device:TPU:8 now
where the time goes in v1:
time: 77.9 us; the launch traced here: 77.7 us
  Pallas kernels  73.6 us (94%)
  local copies, waits for them, and re-layouts  2.84 us (4%)
  between operations  1.29 us (2%)
    pallas_call x1, Pallas kernels, whole_step(): pl.pallas_call(functools.partial(step_kernel, scale), out_shape=(rows, ro...  73.6 us
    unnamed x5, local copies, waits for them, and re-layouts  2.84 us

profile of v1, /device:TPU:8, one launch (start us, length us, event | category | flops | bytes accessed | tf_op | source)
XLA Modules:
  0.0 77.7 jit_solution(229057618574624324)
XLA Ops:
  1.3 0.0 copy-start
  1.3 0.8 %copy-done = f32[9,1024]{1,0:T(8,128)S(1)} copy-done((f32[9,1024]{1,0:T(8,128)S(1)}, f32[9,1024]{1,0:T(8,128)}, u32[]{:S(2)}) %copy-start) | copy-done | bytes 36888
  2.1 73.6 %step.1 = (bf16[1,128,1024]{2,1,0:T(8,128)(2,1)S(1)}, bf16[1,128,1024]{2,1,0:T(8,128)(2,1)S(1)}, f32[32,128]{1,0:T(8,128)S(1)}) custom-call(s32[1]{0:T(128)S(6)} %copy.11.count_ref, bf16[1,128,1024]{2,1,0:T(8,128)(2,1)} %x_hbm.1, bf16[1,128,1024]{2,1,0:T(8,128)(2,1)} %c_hbm.1, f32[9,1024]{1,0:T(8,128)S(1)} %copy-done, bf16[1024,3072]{1,0:T(8,128)(2,1)} %w_hbm.1), custom_call_target="tpu_custom_call" | custom-call | tf_op jit(solution)/shard_map/step/pallas_call | solution.py:448
  75.7 0.7 copy.12
  76.4 0.7 copy.13
  77.1 0.6 copy.14
Async XLA Ops:
  1.3 0.8 %copy-start = (f32[9,1024]{1,0:T(8,128)S(1)}, f32[9,1024]{1,0:T(8,128)}, u32[]{:S(2)}) copy-start(f32[9,1024]{1,0:T(8,128)} %taps_hbm.1) | copy-start | bytes 110596

commit v2 on v1

--- a/solution.py
+++ b/solution.py
@@ -18,7 +18,7 @@
 AHEAD = FRAMES + HALO
 GROWS = FRAMES + 16
 PAIRS = HEADS // 2
-ROWS_A, ROWS_B = 24, 8
+ROWS_A, ROWS_B = 64, 32
 PAIR = 2 * HEAD
 SECTION = 3 * PAIR
 
@@ -44,7 +44,7 @@
     att_ref, gin_ref, out_ref,
     taps_ref, x_own, c_own, xp, xn, cn, ext, hid, slope, cot, mask_own, mask_next, wbuf, qkv, near, gq, gh, gc,
     ht_own, ht_prev, hr_own, hr_prev, g_own, g_prev, gr_own, gr_prev,
-    wa, wb, r_ax, r_by, r_ay, r_bx, r_az, r_bz, local, send, recv,
+    wa, wb, r_ax, r_by, r_ay, r_bx, last, r_z, local, send, recv,
 ):
     tm, dp = lax.axis_index("tm"), lax.axis_index("dp")
     steps = lax.axis_size("tm")
@@ -84,17 +84,6 @@
             wbuf.at[pair, :, pl.ds(section * PAIR, PAIR)],
             local.at[3 + pair * 3 + section],
         )
-
-    own = [
-        pltpu.make_async_copy(x_hbm.at[0], x_own, local.at[0]),
-        pltpu.make_async_copy(c_hbm.at[0], c_own, local.at[1]),
-        pltpu.make_async_copy(taps_hbm, taps_ref, local.at[2]),
-    ]
-    for one in own:
-        one.start()
-    for pair in order:
-        for section in range(3):
-            weight(pair, section).start()
 
     pl.semaphore_wait(barrier, len(peers))
 
@@ -117,7 +106,17 @@
 
     got_xp = start(x_hbm.at[0, pl.ds(FRAMES - HALO, HALO)], xp, after)
     got_xn = start(x_hbm.at[0, pl.ds(0, HALO)], xn, before)
+    own = [
+        pltpu.make_async_copy(x_hbm.at[0], x_own, local.at[0]),
+        pltpu.make_async_copy(taps_hbm, taps_ref, local.at[2]),
+        pltpu.make_async_copy(c_hbm.at[0], c_own, local.at[1]),
+    ]
+    for one in own:
+        one.start()
     got_cn = start(c_hbm.at[0, pl.ds(0, HALO)], cn, before)
+    for pair in order:
+        for section in range(3):
+            weight(pair, section).start()
 
     def live_rows(first, rows):
         at = first + lax.broadcasted_iota(jnp.int32, (rows, 1), 0)
@@ -147,22 +146,20 @@
     def turn(first, take, target):
         for block in range(WIDTH // 128):
             tile = hid[first : first + FRAMES, block * 128 : (block + 1) * 128]
-            turned = tile.astype(jnp.float32).T[:, 0:take]
+            turned = tile.astype(jnp.float32).T.astype(jnp.bfloat16)[:, 0:take]
             for group in range(4):
-                place, side, row = block * 2 + group // 2, group % 2, group * 32
-                at_a, at_b = place * ROWS_A, NX * NZ_HI * ROWS_A + place * ROWS_B
-                target[side, at_a : at_a + ROWS_A, :] = turned[row : row + ROWS_A].astype(jnp.bfloat16)
-                target[side, at_b : at_b + ROWS_B, :] = turned[row + ROWS_A : row + 32].astype(jnp.bfloat16)
+                place, side = (block * 2 + group // 2) * 32, group % 2
+                target[side, place : place + 32, :] = turned[group * 32 : (group + 1) * 32]
 
     inner = HALO + 16
     ext[0:8, :] = jnp.zeros((8, WIDTH), jnp.float32)
     mask_own[...] = band(FRAMES, AHEAD, begin, begin - HALO)
     mask_next[...] = band(HALO, 2 * HALO, begin + FRAMES, begin + FRAMES - HALO)
     own[0].wait()
-    own[2].wait()
+    own[1].wait()
     ext[8 + HALO : 8 + AHEAD, :] = masked(begin, x_own[...])
     lax.fori_loop(inner // 16, AHEAD // 16, conv_rows, 0)
-    own[1].wait()
+    own[2].wait()
     cot[0:FRAMES, :] = masked(begin, c_own[...]).astype(jnp.bfloat16)
     for pair in order:
         for section in range(3):
@@ -232,18 +229,18 @@
                     jnp.concatenate([hr_own[...], hr_prev[...]], axis=1),
                     jnp.concatenate([gr_own[turn_no, :, at], gr_prev[turn_no, :, low]], axis=0),
                 )
+            product = product.astype(jnp.bfloat16)
             for row in range(NX):
                 for high in range(NZ_HI):
-                    place = row * NZ_HI + high
-                    at_a, at_b = place * ROWS_A, NX * NZ_HI * ROWS_A + place * ROWS_B
+                    first = (row * NZ_HI + high) * 32
                     for head in range(2):
-                        lane = slice(head * HEAD, (head + 1) * HEAD)
-                        wa[row, pair * 2 + head, high * NZ_LO + section] = product[
-                            at_a : at_a + ROWS_A, lane
-                        ].astype(jnp.bfloat16)
-                        wb[pair * 2 + head, row, high * NZ_LO + section] = product[
-                            at_b : at_b + ROWS_B, lane
-                        ].astype(jnp.bfloat16)
+                        value = product[first : first + 32, head * HEAD : (head + 1) * HEAD]
+                        if section == 0:
+                            wa[row, pair * 2 + head, high, 0:32, :] = value
+                        else:
+                            at_a, at_b = 16 + section * 16, section * 16 - 16
+                            wa[row, pair * 2 + head, high, at_a : at_a + 16, :] = value[0:16]
+                            wb[pair * 2 + head, row, high, at_b : at_b + 16, :] = value[16:32]
 
     def add_into(ref, landed):
         total = ref[...].astype(jnp.float32)
@@ -298,10 +295,10 @@
         return half(wb.at[place], which, NX)
 
     def ay_block(place, which):
-        return half(wa.at[x, place], which, NZ)
+        return half(wa.at[x, place], which, NZ_HI)
 
     def bx_block(place, which):
-        return half(wb.at[y, place], which, NZ)
+        return half(wb.at[y, place], which, NZ_HI)
 
     by = four("y", NY, y, by_block, r_by)
     ay = four("y", NY, y, ay_block, r_ay)
@@ -353,21 +350,27 @@
         gc[...] = gh[...] * slope[HALO : HALO + GROWS, :]
         lax.fori_loop(0, FRAMES // 16, spread_rows, 0)
 
-    def send_column(block, landing):
-        return [
-            start(block.at[lax.rem(z + k, NZ)], landing.at[k - 1], column[k - 1]) for k in range(1, NZ)
-        ]
-
-    def finish(rows, own_block, landing, landed):
-        total = own_block[z].astype(jnp.float32)
-        for index, one in enumerate(landed):
-            one.wait_recv()
-            total = total + landing[index].astype(jnp.float32)
-        out_ref[rows, :] = total * scale
-
-    def finish_ax(turn_no):
+    def send_column():
+        for high in range(NZ_HI):
+            last[high * NZ_LO] = wa[x, y, high, 0:32, :]
+            for section in range(1, NZ_LO):
+                at_a, at_b = 16 + section * 16, section * 16 - 16
+                last[high * NZ_LO + section, 0:16, :] = wa[x, y, high, at_a : at_a + 16, :]
+                last[high * NZ_LO + section, 16:32, :] = wb[y, x, high, at_b : at_b + 16, :]
+        far_first = sorted(range(1, NZ), key=lambda k: abs(k - NZ // 2))
+        return {k: start(last.at[lax.rem(z + k, NZ)], r_z.at[k - 1], column[k - 1]) for k in far_first}
+
+    def finish(landed):
+        total = last[z].astype(jnp.float32)
+        for k in sorted(landed, key=lambda k: -abs(k - NZ // 2)):
+            landed[k].wait_recv()
+            total = total + r_z[k - 1].astype(jnp.float32)
+        out_ref[...] = total * scale
+
+    def finish_ax(turn_no, heads=(0, 1)):
         chains, block = ax[turn_no]
-        finish_four(chains, block, x)
+        for head in heads:
+            add_into(block(x, head), [chains[head].last(), chains[3 - head].last()])
 
     sent_0 = attend_own(0)
     sent_1 = attend_own(1)
@@ -379,44 +382,46 @@
     sent_2 = attend_own(2)
     products(1, sent_1)
     step_all(ax[1][0], (0, 1, 2, 3))
+    sent_3 = attend_own(3)
+    step_all(ax[0][0], (0, 1))
     step_all(by, (0, 2))
-    step_all(ax[0][0], (0, 1))
-    sent_3 = attend_own(3)
     products(2, sent_2)
-    step_all(ax[2][0], (0, 1, 2, 3))
-    step_all(by, (1, 3, 0, 2))
+    step_all(ax[2][0], (0, 1, 3, 2))
+    step_all(by, (1, 3))
     products(3, sent_3)
+    step_all(by, (0,))
     step_all(ax[1][0], (0, 1))
-    step_all(ax[3][0], (0, 1, 2, 3))
-    step_all(by, (1, 3, 0, 2))
+    step_all(ax[3][0], (0, 1))
+    step_all(by, (2, 1))
     conv_next()
-    step_all(ax[2][0], (0, 1))
-    step_all(by, (1, 3))
-    attend_next(0)
+    step_all(by, (3,))
     finish_ax(0)
     step_all(ay, (0, 1))
+    step_all(ax[2][0], (0, 1))
+    step_all(ax[3][0], (2, 3))
+    step_all(by, (0,))
+    attend_next(0)
+    step_all(by, (2, 1))
+    finish_ax(1)
+    step_all(ay, (0, 2))
+    step_all(by, (3,))
+    attend_next(1)
     step_all(ax[3][0], (0, 1))
-    attend_next(1)
+    finish_ax(2)
+    step_all(ay, (1, 3, 0, 2))
     finish_four(by, by_block, y)
     step_all(bx, (0, 1, 2, 3))
-    finish_ax(1)
-    step_all(ay, (0, 2))
+    step_all(ay, (1, 3))
+    step_all(bx, (0, 1))
+    finish_ax(3)
+    step_all(ay, (0, 2, 1, 3))
+    finish_four(bx, bx_block, x)
+    finish_four(ay, ay_block, y)
+    landed = send_column()
     attend_next(2)
-    step_all(ay, (0, 2))
-    step_all(bx, (0, 1))
-    finish_ax(2)
-    step_all(ay, (1, 3))
     attend_next(3)
-    step_all(ay, (1, 3))
-    finish_four(bx, bx_block, x)
-    got_b = send_column(wb.at[y, x], r_bz)
-    finish_ax(3)
-    step_all(ay, (0, 1, 2, 3))
     spread()
-    finish_four(ay, ay_block, y)
-    got_a = send_column(wa.at[x, y], r_az)
-    finish(slice(ROWS_A, ROWS_A + ROWS_B), wb.at[y, x], r_bz, got_b)
-    finish(slice(0, ROWS_A), wa.at[x, y], r_az, got_a)
+    finish(landed)
     for one in sent:
         one.wait_send()
 
@@ -440,10 +445,10 @@
         ((WIDTH // 2, FRAMES), bf16), ((WIDTH // 2, HALO), bf16),
         ((PAIRS, FRAMES, SECTION), bf16), ((PAIRS, HALO, 2 * PAIR), bf16),
         ((PAIRS, FRAMES, SECTION), bf16), ((PAIRS, HALO, 2 * PAIR), bf16),
-        ((NX, NY, NZ, ROWS_A, HEAD), bf16), ((NY, NX, NZ, ROWS_B, HEAD), bf16),
-        ((PAIRS, 6, NZ, ROWS_A, HEAD), bf16), ((14, NX // 2, NZ, ROWS_B, HEAD), bf16),
-        ((14, NZ // 2, ROWS_A, HEAD), bf16), ((6, NZ // 2, ROWS_B, HEAD), bf16),
-        ((NZ - 1, ROWS_A, HEAD), bf16), ((NZ - 1, ROWS_B, HEAD), bf16),
+        ((NX, NY, NZ_HI, ROWS_A, HEAD), bf16), ((NY, NX, NZ_HI, ROWS_B, HEAD), bf16),
+        ((PAIRS, 6, NZ_HI, ROWS_A, HEAD), bf16), ((14, NX // 2, NZ_HI, ROWS_B, HEAD), bf16),
+        ((14, NZ_HI // 2, ROWS_A, HEAD), bf16), ((6, NZ_HI // 2, ROWS_B, HEAD), bf16),
+        ((NZ, 32, HEAD), bf16), ((NZ - 1, 32, HEAD), bf16),
     ]
     return pl.pallas_call(
         functools.partial(step_kernel, scale),

time: 77.9 us -> 71.8 us (0.922)
  Pallas kernels: 73.6 us -> 67.5 us
    pallas_call x1, Pallas kernels: 73.6 us -> 67.5 us  [whole_step(): pl.pallas_call(functools.partial(step_kernel, scale), out_shape=(rows, ro...]
where the time goes in v2:
time: 71.8 us; the launch traced here: 71.6 us
  Pallas kernels  67.5 us (94%)
  local copies, waits for them, and re-layouts  2.84 us (4%)
  between operations  1.29 us (2%)
    pallas_call x1, Pallas kernels, whole_step(): pl.pallas_call(functools.partial(step_kernel, scale), out_shape=(rows, ro...  67.5 us
    unnamed x5, local copies, waits for them, and re-layouts  2.84 us

profile of v2, /device:TPU:8, one launch (start us, length us, event | category | flops | bytes accessed | tf_op | source)
XLA Modules:
  0.0 71.6 jit_solution(4201437681425260994)
XLA Ops:
  1.3 0.0 copy-start
  1.3 0.8 %copy-done = f32[9,1024]{1,0:T(8,128)S(1)} copy-done((f32[9,1024]{1,0:T(8,128)S(1)}, f32[9,1024]{1,0:T(8,128)}, u32[]{:S(2)}) %copy-start) | copy-done | bytes 36888
  2.1 67.5 %step.1 = (bf16[1,128,1024]{2,1,0:T(8,128)(2,1)S(1)}, bf16[1,128,1024]{2,1,0:T(8,128)(2,1)S(1)}, f32[32,128]{1,0:T(8,128)S(1)}) custom-call(s32[1]{0:T(128)S(6)} %copy.11.count_ref, bf16[1,128,1024]{2,1,0:T(8,128)(2,1)} %x_hbm.1, bf16[1,128,1024]{2,1,0:T(8,128)(2,1)} %c_hbm.1, f32[9,1024]{1,0:T(8,128)S(1)} %copy-done, bf16[1024,3072]{1,0:T(8,128)(2,1)} %w_hbm.1), custom_call_target="tpu_custom_call" | custom-call | tf_op jit(solution)/shard_map/step/pallas_call | solution.py:453
  69.6 0.7 copy.12
  70.3 0.7 copy.13
  71.0 0.6 copy.14
Async XLA Ops:
  1.3 0.8 %copy-start = (f32[9,1024]{1,0:T(8,128)S(1)}, f32[9,1024]{1,0:T(8,128)}, u32[]{:S(2)}) copy-start(f32[9,1024]{1,0:T(8,128)} %taps_hbm.1) | copy-start | bytes 110596

commit v3 on v2

--- a/solution.py
+++ b/solution.py
@@ -41,8 +41,8 @@
 
 def step_kernel(
     scale, count_ref, x_hbm, c_hbm, taps_hbm, w_hbm,
-    att_ref, gin_ref, out_ref,
-    taps_ref, x_own, c_own, xp, xn, cn, ext, hid, slope, cot, mask_own, mask_next, wbuf, qkv, near, gq, gh, gc,
+    att_out, gin_out, sum_out,
+    att_ref, gin_ref, out_ref, taps_ref, x_own, c_own, xp, xn, cn, ext, hid, slope, cot, mask_own, mask_next, wbuf, qkv, near, gq, gh, gc,
     ht_own, ht_prev, hr_own, hr_prev, g_own, g_prev, gr_own, gr_prev,
     wa, wb, r_ax, r_by, r_ay, r_bx, last, r_z, local, send, recv,
 ):
@@ -72,7 +72,8 @@
     column = [device(x, y, lax.rem(z + k, NZ), core) for k in range(1, NZ)]
 
     barrier = pltpu.get_barrier_semaphore()
-    peers = [after, before, *near_by.values(), *column]
+    row = [device(lax.rem(x + k, NX), y, z, core) for k in range(1, NX)]
+    peers = [after, before, *near_by.values(), row[1], *column]
     for other in peers:
         pl.semaphore_signal(barrier, inc=1, device_id=other, device_id_type=MESH)
 
@@ -82,30 +83,31 @@
         return pltpu.make_async_copy(
             w_hbm.at[:, pl.ds(section * WIDTH + pair * PAIR, PAIR)],
             wbuf.at[pair, :, pl.ds(section * PAIR, PAIR)],
-            local.at[3 + pair * 3 + section],
+            local.at[3 + pair],
         )
 
     pl.semaphore_wait(barrier, len(peers))
 
     slots = iter(range(SLOTS))
-    sent = []
-
-    def start(source, target, other):
-        slot = next(slots)
-        one = pltpu.make_async_remote_copy(
+    groups = [xp, xn, cn, hr_own, hr_prev, gr_own, gr_prev, r_ax, r_by, r_ay, r_bx, r_z]
+
+    def describe(source, target, group, slot, other):
+        return pltpu.make_async_remote_copy(
             src_ref=source,
             dst_ref=target,
-            send_sem=send.at[slot],
+            send_sem=send.at[group],
             recv_sem=recv.at[slot],
             device_id=other,
             device_id_type=MESH,
         )
+
+    def start(source, target, other, group, slot=None):
+        one = describe(source, target, group, next(slots) if slot is None else slot, other)
         one.start()
-        sent.append(one)
         return one
 
-    got_xp = start(x_hbm.at[0, pl.ds(FRAMES - HALO, HALO)], xp, after)
-    got_xn = start(x_hbm.at[0, pl.ds(0, HALO)], xn, before)
+    got_xp = start(x_hbm.at[0, pl.ds(FRAMES - HALO, HALO)], xp, after, 0)
+    got_xn = start(x_hbm.at[0, pl.ds(0, HALO)], xn, before, 1)
     own = [
         pltpu.make_async_copy(x_hbm.at[0], x_own, local.at[0]),
         pltpu.make_async_copy(taps_hbm, taps_ref, local.at[2]),
@@ -113,7 +115,7 @@
     ]
     for one in own:
         one.start()
-    got_cn = start(c_hbm.at[0, pl.ds(0, HALO)], cn, before)
+    got_cn = start(c_hbm.at[0, pl.ds(0, HALO)], cn, before, 2)
     for pair in order:
         for section in range(3):
             weight(pair, section).start()
@@ -162,8 +164,7 @@
     own[2].wait()
     cot[0:FRAMES, :] = masked(begin, c_own[...]).astype(jnp.bfloat16)
     for pair in order:
-        for section in range(3):
-            weight(pair, section).wait()
+        pltpu.make_async_copy(wbuf.at[pair], wbuf.at[pair], local.at[3 + pair]).wait()
         qkv[pair, inner:AHEAD, :] = dot_nn(hid[inner:AHEAD, :], wbuf[pair]).astype(jnp.bfloat16)
 
     got_xp.wait_recv()
@@ -171,7 +172,10 @@
     lax.fori_loop(0, inner // 16, conv_rows, 0)
     turn(HALO, FRAMES, ht_own)
     turn(0, HALO, ht_prev)
-    got_h = [start(ht_own.at[1 - core], hr_own, partner), start(ht_prev.at[1 - core], hr_prev, partner)]
+    got_h = [
+        start(ht_own.at[1 - core], hr_own, partner, 3),
+        start(ht_prev.at[1 - core], hr_prev, partner, 4),
+    ]
 
     def attend(q, g, k, v, mask, first):
         raised = jnp.where(mask > 0.5, jnp.exp(dot_nt(q, k) * factor), 0.0)
@@ -206,8 +210,8 @@
                 g_own[turn_no, :, section_at(section, head)] = total[HALO:AHEAD].astype(jnp.bfloat16)
                 near[turn_no, :, section_at(section - 1, head)] = total[HALO:AHEAD]
         return [
-            start(g_own.at[turn_no], gr_own.at[turn_no], partner),
-            start(g_prev.at[turn_no], gr_prev.at[turn_no], partner),
+            start(g_own.at[turn_no], gr_own.at[turn_no], partner, 5),
+            start(g_prev.at[turn_no], gr_prev.at[turn_no], partner, 6),
         ]
 
     def products(turn_no, landed):
@@ -249,7 +253,8 @@
         ref[...] = total.astype(jnp.bfloat16)
 
     class Chain:
-        def __init__(self, axis, size, at, way, length, block, landing):
+        def __init__(self, group, axis, size, at, way, length, block, landing):
+            self.group = group
             self.to, self.size, self.at, self.way, self.length = near_by[axis, way], size, at, way, length
             self.block, self.landing, self.done, self.pending = block, landing, 0, None
 
@@ -260,7 +265,7 @@
             if self.pending is not None:
                 self.pending.wait_recv()
                 add_into(ref, [self.landing(self.done - 2)])
-            self.pending = start(ref, self.landing(self.done - 1), self.to)
+            self.pending = start(ref, self.landing(self.done - 1), self.to, self.group)
 
         def last(self):
             self.pending.wait_recv()
@@ -269,12 +274,12 @@
     def half(ref, which, size):
         return ref.at[pl.ds(which * (size // 2), size // 2)]
 
-    def four(axis, size, at, block, landing):
+    def four(group, axis, size, at, block, landing):
         far, less = size // 2, size // 2 - 1
         chains, slot = [], 0
         for way, which, length in ((1, 0, far), (-1, 1, far), (1, 1, less), (-1, 0, less)):
             chains.append(
-                Chain(axis, size, at, way, length,
+                Chain(group, axis, size, at, way, length,
                       lambda place, which=which: block(place, which),
                       lambda step, slot=slot: landing.at[slot + step])
             )
@@ -289,7 +294,7 @@
     for turn_no in range(PAIRS):
         def head_block(place, which, turn_no=turn_no):
             return wa.at[place, order[turn_no] * 2 + which]
-        ax.append((four("x", NX, x, head_block, r_ax.at[turn_no]), head_block))
+        ax.append((four(7, "x", NX, x, head_block, r_ax.at[turn_no]), head_block))
 
     def by_block(place, which):
         return half(wb.at[place], which, NX)
@@ -297,12 +302,8 @@
     def ay_block(place, which):
         return half(wa.at[x, place], which, NZ_HI)
 
-    def bx_block(place, which):
-        return half(wb.at[y, place], which, NZ_HI)
-
-    by = four("y", NY, y, by_block, r_by)
-    ay = four("y", NY, y, ay_block, r_ay)
-    bx = four("x", NX, x, bx_block, r_bx)
+    by = four(8, "y", NY, y, by_block, r_by)
+    ay = four(9, "y", NY, y, ay_block, r_ay)
 
     def step_all(chains, which):
         for index in which:
@@ -350,6 +351,14 @@
         gc[...] = gh[...] * slope[HALO : HALO + GROWS, :]
         lax.fori_loop(0, FRAMES // 16, spread_rows, 0)
 
+    def send_row():
+        for k in (2, 1, 3):
+            start(wb.at[y, lax.rem(x + k, NX)], r_bx.at[k - 1], row[k - 1], 10, SLOTS)
+
+    def finish_row():
+        describe(r_bx, r_bx, 10, SLOTS, partner).wait_recv()
+        add_into(wb.at[y, x], [r_bx.at[k] for k in range(NX - 1)])
+
     def send_column():
         for high in range(NZ_HI):
             last[high * NZ_LO] = wa[x, y, high, 0:32, :]
@@ -358,13 +367,14 @@
                 last[high * NZ_LO + section, 0:16, :] = wa[x, y, high, at_a : at_a + 16, :]
                 last[high * NZ_LO + section, 16:32, :] = wb[y, x, high, at_b : at_b + 16, :]
         far_first = sorted(range(1, NZ), key=lambda k: abs(k - NZ // 2))
-        return {k: start(last.at[lax.rem(z + k, NZ)], r_z.at[k - 1], column[k - 1]) for k in far_first}
-
-    def finish(landed):
+        for k in far_first:
+            start(last.at[lax.rem(z + k, NZ)], r_z.at[k - 1], column[k - 1], 11, SLOTS + 1)
+
+    def finish():
+        describe(r_z, r_z, 11, SLOTS + 1, partner).wait_recv()
         total = last[z].astype(jnp.float32)
-        for k in sorted(landed, key=lambda k: -abs(k - NZ // 2)):
-            landed[k].wait_recv()
-            total = total + r_z[k - 1].astype(jnp.float32)
+        for k in range(NZ - 1):
+            total = total + r_z[k].astype(jnp.float32)
         out_ref[...] = total * scale
 
     def finish_ax(turn_no, heads=(0, 1)):
@@ -383,58 +393,64 @@
     products(1, sent_1)
     step_all(ax[1][0], (0, 1, 2, 3))
     sent_3 = attend_own(3)
+    results = [pltpu.make_async_copy(att_ref, att_out, local.at[3 + PAIRS])]
+    results[0].start()
     step_all(ax[0][0], (0, 1))
     step_all(by, (0, 2))
     products(2, sent_2)
-    step_all(ax[2][0], (0, 1, 3, 2))
+    step_all(ax[2][0], (0, 1))
     step_all(by, (1, 3))
     products(3, sent_3)
-    step_all(by, (0,))
     step_all(ax[1][0], (0, 1))
-    step_all(ax[3][0], (0, 1))
-    step_all(by, (2, 1))
+    step_all(ax[2][0], (3, 2))
+    step_all(by, (0, 2, 1))
     conv_next()
-    step_all(by, (3,))
     finish_ax(0)
     step_all(ay, (0, 1))
     step_all(ax[2][0], (0, 1))
-    step_all(ax[3][0], (2, 3))
-    step_all(by, (0,))
+    step_all(ax[3][0], (0, 1, 3, 2))
+    step_all(by, (3, 0))
     attend_next(0)
-    step_all(by, (2, 1))
     finish_ax(1)
     step_all(ay, (0, 2))
-    step_all(by, (3,))
-    attend_next(1)
+    step_all(by, (2, 1, 3))
+    finish_ax(2)
+    step_all(ay, (1, 3))
     step_all(ax[3][0], (0, 1))
-    finish_ax(2)
-    step_all(ay, (1, 3, 0, 2))
+    step_all(ay, (0, 2))
     finish_four(by, by_block, y)
-    step_all(bx, (0, 1, 2, 3))
+    send_row()
     step_all(ay, (1, 3))
-    step_all(bx, (0, 1))
     finish_ax(3)
     step_all(ay, (0, 2, 1, 3))
-    finish_four(bx, bx_block, x)
+    finish_row()
     finish_four(ay, ay_block, y)
-    landed = send_column()
+    send_column()
+    attend_next(1)
     attend_next(2)
     attend_next(3)
     spread()
-    finish(landed)
-    for one in sent:
-        one.wait_send()
-
-
-SLOTS = 112
+    results.append(pltpu.make_async_copy(gin_ref, gin_out, local.at[4 + PAIRS]))
+    results[1].start()
+    finish()
+    results.append(pltpu.make_async_copy(out_ref, sum_out, local.at[5 + PAIRS]))
+    results[2].start()
+    for one in results:
+        one.wait()
+    for group, whole in enumerate(groups):
+        describe(whole, whole, group, 0, partner).wait_send()
+
+
+SLOTS = 65
 
 
 def whole_step(frames_in, valid_frames, taps, w_qkv, cotangent):
-    vmem, anywhere = pl.BlockSpec(memory_space=pltpu.VMEM), pl.BlockSpec(memory_space=pl.ANY)
+    anywhere = pl.BlockSpec(memory_space=pl.ANY)
     bf16, f32 = jnp.bfloat16, jnp.float32
     rows = jax.ShapeDtypeStruct((1, FRAMES, WIDTH), bf16)
     scale = float(lax.axis_size("dp") * lax.axis_size("tm") * FRAMES) ** (-0.5)
     scratch = [
+        ((1, FRAMES, WIDTH), bf16), ((1, FRAMES, WIDTH), bf16), ((32, HEAD), f32),
         ((KERNEL, WIDTH), f32), ((FRAMES, WIDTH), bf16), ((FRAMES, WIDTH), bf16),
         ((HALO, WIDTH), bf16), ((HALO, WIDTH), bf16), ((HALO, WIDTH), bf16),
         ((EXT + 8, WIDTH), f32), ((EXT, WIDTH), bf16), ((EXT, WIDTH), f32), ((AHEAD, WIDTH), bf16),
@@ -447,16 +463,16 @@
         ((PAIRS, FRAMES, SECTION), bf16), ((PAIRS, HALO, 2 * PAIR), bf16),
         ((NX, NY, NZ_HI, ROWS_A, HEAD), bf16), ((NY, NX, NZ_HI, ROWS_B, HEAD), bf16),
         ((PAIRS, 6, NZ_HI, ROWS_A, HEAD), bf16), ((14, NX // 2, NZ_HI, ROWS_B, HEAD), bf16),
-        ((14, NZ_HI // 2, ROWS_A, HEAD), bf16), ((6, NZ_HI // 2, ROWS_B, HEAD), bf16),
+        ((14, NZ_HI // 2, ROWS_A, HEAD), bf16), ((NX - 1, NZ_HI, ROWS_B, HEAD), bf16),
         ((NZ, 32, HEAD), bf16), ((NZ - 1, 32, HEAD), bf16),
     ]
     return pl.pallas_call(
         functools.partial(step_kernel, scale),
         out_shape=(rows, rows, jax.ShapeDtypeStruct((32, HEAD), f32)),
         in_specs=[pl.BlockSpec(memory_space=pltpu.SMEM)] + [anywhere] * 4,
-        out_specs=(vmem, vmem, vmem),
+        out_specs=(anywhere,) * 3,
         scratch_shapes=[pltpu.VMEM(shape, kind) for shape, kind in scratch]
-        + [pltpu.SemaphoreType.DMA((3 + 3 * PAIRS,)), pltpu.SemaphoreType.DMA((SLOTS,)), pltpu.SemaphoreType.DMA((SLOTS,))],
+        + [pltpu.SemaphoreType.DMA((6 + PAIRS,)), pltpu.SemaphoreType.DMA((12,)), pltpu.SemaphoreType.DMA((SLOTS + 2,))],
         compiler_params=pltpu.CompilerParams(
             collective_id=0, has_side_effects=True, vmem_limit_bytes=54500 * 1024
         ),

time: 71.8 us -> 69.3 us (0.965)
  Pallas kernels: 67.5 us -> 65 us
    pallas_call x1, Pallas kernels: 67.5 us -> 65 us  [whole_step(): pl.pallas_call(functools.partial(step_kernel, scale), out_shape=(rows, ro...]
where the time goes in v3:
time: 69.3 us; the launch traced here: 69.1 us
  Pallas kernels  65 us (94%)
  local copies, waits for them, and re-layouts  2.84 us (4%)
  between operations  1.29 us (2%)
    pallas_call x1, Pallas kernels, whole_step(): pl.pallas_call(functools.partial(step_kernel, scale), out_shape=(rows, ro...  65 us
    unnamed x5, local copies, waits for them, and re-layouts  2.84 us

profile of v3, /device:TPU:8, one launch (start us, length us, event | category | flops | bytes accessed | tf_op | source)
XLA Modules:
  0.0 69.1 jit_solution(8849284442649044369)
XLA Ops:
  1.3 0.0 copy-start
  1.3 0.8 %copy-done = f32[9,1024]{1,0:T(8,128)S(1)} copy-done((f32[9,1024]{1,0:T(8,128)S(1)}, f32[9,1024]{1,0:T(8,128)}, u32[]{:S(2)}) %copy-start) | copy-done | bytes 36888
  2.1 65.0 %step.1 = (bf16[1,128,1024]{2,1,0:T(8,128)(2,1)S(1)}, bf16[1,128,1024]{2,1,0:T(8,128)(2,1)S(1)}, f32[32,128]{1,0:T(8,128)S(1)}) custom-call(s32[1]{0:T(128)S(6)} %copy.11.count_ref, bf16[1,128,1024]{2,1,0:T(8,128)(2,1)} %x_hbm.1, bf16[1,128,1024]{2,1,0:T(8,128)(2,1)} %c_hbm.1, f32[9,1024]{1,0:T(8,128)S(1)} %copy-done, bf16[1024,3072]{1,0:T(8,128)(2,1)} %w_hbm.1), custom_call_target="tpu_custom_call" | custom-call | tf_op jit(solution)/shard_map/step/pallas_call | solution.py:469
  67.1 0.7 %copy.12 = bf16[1,128,1024]{2,1,0:T(8,128)(2,1)} copy(bf16[1,128,1024]{2,1,0:T(8,128)(2,1)S(1)} %get-tuple-element.12) | data formatting | bytes 524288
  67.8 0.7 %copy.13 = bf16[1,128,1024]{2,1,0:T(8,128)(2,1)} copy(bf16[1,128,1024]{2,1,0:T(8,128)(2,1)S(1)} %get-tuple-element.13) | data formatting | bytes 524288
  68.5 0.6 copy.14
Async XLA Ops:
  1.3 0.8 %copy-start = (f32[9,1024]{1,0:T(8,128)S(1)}, f32[9,1024]{1,0:T(8,128)}, u32[]{:S(2)}) copy-start(f32[9,1024]{1,0:T(8,128)} %taps_hbm.1) | copy-start | bytes 110596

commit v4 on v3

--- a/solution.py
+++ b/solution.py
@@ -18,7 +18,8 @@
 AHEAD = FRAMES + HALO
 GROWS = FRAMES + 16
 PAIRS = HEADS // 2
-ROWS_A, ROWS_B = 64, 32
+ROWS_A, ROWS_B = 56, 40
+PLACES = ((0, 0, 24), (24, 8, 16), (40, 24, 16))
 PAIR = 2 * HEAD
 SECTION = 3 * PAIR
 
@@ -233,18 +234,14 @@
                     jnp.concatenate([hr_own[...], hr_prev[...]], axis=1),
                     jnp.concatenate([gr_own[turn_no, :, at], gr_prev[turn_no, :, low]], axis=0),
                 )
-            product = product.astype(jnp.bfloat16)
             for row in range(NX):
                 for high in range(NZ_HI):
                     first = (row * NZ_HI + high) * 32
                     for head in range(2):
                         value = product[first : first + 32, head * HEAD : (head + 1) * HEAD]
-                        if section == 0:
-                            wa[row, pair * 2 + head, high, 0:32, :] = value
-                        else:
-                            at_a, at_b = 16 + section * 16, section * 16 - 16
-                            wa[row, pair * 2 + head, high, at_a : at_a + 16, :] = value[0:16]
-                            wb[pair * 2 + head, row, high, at_b : at_b + 16, :] = value[16:32]
+                        at_a, at_b, cut = PLACES[section]
+                        wa[row, pair * 2 + head, high, at_a : at_a + cut, :] = value[0:cut].astype(jnp.bfloat16)
+                        wb[pair * 2 + head, row, high, at_b : at_b + 32 - cut, :] = value[cut:32].astype(jnp.bfloat16)
 
     def add_into(ref, landed):
         total = ref[...].astype(jnp.float32)
@@ -361,11 +358,9 @@
 
     def send_column():
         for high in range(NZ_HI):
-            last[high * NZ_LO] = wa[x, y, high, 0:32, :]
-            for section in range(1, NZ_LO):
-                at_a, at_b = 16 + section * 16, section * 16 - 16
-                last[high * NZ_LO + section, 0:16, :] = wa[x, y, high, at_a : at_a + 16, :]
-                last[high * NZ_LO + section, 16:32, :] = wb[y, x, high, at_b : at_b + 16, :]
+            for section, (at_a, at_b, cut) in enumerate(PLACES):
+                last[high * NZ_LO + section, 0:cut, :] = wa[x, y, high, at_a : at_a + cut, :]
+                last[high * NZ_LO + section, cut:32, :] = wb[y, x, high, at_b : at_b + 32 - cut, :]
         far_first = sorted(range(1, NZ), key=lambda k: abs(k - NZ // 2))
         for k in far_first:
             start(last.at[lax.rem(z + k, NZ)], r_z.at[k - 1], column[k - 1], 11, SLOTS + 1)
@@ -392,35 +387,37 @@
     sent_2 = attend_own(2)
     products(1, sent_1)
     step_all(ax[1][0], (0, 1, 2, 3))
+    step_all(by, (2,))
     sent_3 = attend_own(3)
     results = [pltpu.make_async_copy(att_ref, att_out, local.at[3 + PAIRS])]
     results[0].start()
     step_all(ax[0][0], (0, 1))
-    step_all(by, (0, 2))
+    step_all(by, (0,))
     products(2, sent_2)
     step_all(ax[2][0], (0, 1))
     step_all(by, (1, 3))
     products(3, sent_3)
     step_all(ax[1][0], (0, 1))
     step_all(ax[2][0], (3, 2))
-    step_all(by, (0, 2, 1))
+    step_all(by, (2,))
     conv_next()
+    step_all(by, (0, 1))
     finish_ax(0)
     step_all(ay, (0, 1))
     step_all(ax[2][0], (0, 1))
     step_all(ax[3][0], (0, 1, 3, 2))
-    step_all(by, (3, 0))
+    step_all(by, (3, 2))
     attend_next(0)
+    step_all(by, (0, 1))
     finish_ax(1)
     step_all(ay, (0, 2))
-    step_all(by, (2, 1, 3))
     finish_ax(2)
     step_all(ay, (1, 3))
+    step_all(by, (3,))
     step_all(ax[3][0], (0, 1))
-    step_all(ay, (0, 2))
+    step_all(ay, (0, 2, 1, 3))
     finish_four(by, by_block, y)
     send_row()
-    step_all(ay, (1, 3))
     finish_ax(3)
     step_all(ay, (0, 2, 1, 3))
     finish_row()
@@ -477,7 +474,7 @@
             collective_id=0, has_side_effects=True, vmem_limit_bytes=54500 * 1024
         ),
         name="step",
-    )(valid_frames, frames_in, cotangent, taps, w_qkv)
+    )(valid_frames, *(pltpu.with_memory_space_constraint(one, pltpu.HBM) for one in (frames_in, cotangent, taps, w_qkv)))
 
 
 def on_device(frames_in, valid_frames, kernel, w_qkv, cotangent):

time: 69.3 us -> 66.3 us (0.957)
  Pallas kernels: 65 us -> 62.8 us
  local copies, waits for them, and re-layouts: 2.84 us -> 2.01 us
    pallas_call x1, Pallas kernels: 65 us -> 62.8 us  [whole_step(): pl.pallas_call(functools.partial(step_kernel, scale), out_shape=(rows, ro...]
    unnamed x5 -> x3, local copies, waits for them, and re-layouts: 2.84 us -> 2.01 us
where the time goes in v4:
time: 66.3 us; the launch traced here: 66.1 us
  Pallas kernels  62.8 us (95%)
  local copies, waits for them, and re-layouts  2.01 us (3%)
  between operations  1.29 us (2%)
    pallas_call x1, Pallas kernels, whole_step(): pl.pallas_call(functools.partial(step_kernel, scale), out_shape=(rows, ro...  62.8 us
    unnamed x3, local copies, waits for them, and re-layouts  2.01 us

profile of v4, /device:TPU:8, one launch (start us, length us, event | category | flops | bytes accessed | tf_op | source)
XLA Modules:
  0.0 66.1 jit_solution(12200482895734199176)
XLA Ops:
  1.3 62.8 %step.1 = (bf16[1,128,1024]{2,1,0:T(8,128)(2,1)S(1)}, bf16[1,128,1024]{2,1,0:T(8,128)(2,1)S(1)}, f32[32,128]{1,0:T(8,128)S(1)}) custom-call(s32[1]{0:T(128)S(6)} %copy.11.count_ref, bf16[1,128,1024]{2,1,0:T(8,128)(2,1)} %x_hbm.1, bf16[1,128,1024]{2,1,0:T(8,128)(2,1)} %c_hbm.1, f32[9,1024]{1,0:T(8,128)} %taps_hbm.1, bf16[1024,3072]{1,0:T(8,128)(2,1)} %w_hbm.1), custom_call_target="tpu_custom_call" | custom-call | tf_op jit(solution)/shard_map/step/pallas_call | solution.py:466
  64.1 0.7 %copy.12 = bf16[1,128,1024]{2,1,0:T(8,128)(2,1)} copy(bf16[1,128,1024]{2,1,0:T(8,128)(2,1)S(1)} %get-tuple-element.12) | data formatting | bytes 524288
  64.8 0.7 %copy.13 = bf16[1,128,1024]{2,1,0:T(8,128)(2,1)} copy(bf16[1,128,1024]{2,1,0:T(8,128)(2,1)S(1)} %get-tuple-element.13) | data formatting | bytes 524288
  65.5 0.6 copy.14
